TPU v7x, 32 devices: a whole 2x2x4 slice. The times are simulated.
32 devices in a mesh: dp: 16 (over z, y, x), tensor: 2 (over core).
Axes of the slice: x: 2, y: 2, z: 4, core: 2. Of those that a mesh axis runs over, the one named last changes fastest.
Arguments:
- inputs: bfloat16 [8192, 2048], P('dp'), may hold values from -6 to 6
- gamma_first: bfloat16 [2048], replicated, may hold values from 0.099609375 to 1.8984375
- beta_first: bfloat16 [2048], replicated, may hold values from -4 to 4
- heads_weight: bfloat16 [2048, 3, 2048], P('dp', None, 'tensor'), may hold values from -0.125 to 0.125
- output_weight: bfloat16 [2048, 2048], P('dp', 'tensor'), may hold values from -0.5 to 0.5
- output_bias: bfloat16 [2048], replicated, may hold values from -4 to 4
- gamma_second: bfloat16 [2048], replicated, may hold values from 0.099609375 to 1.8984375
- beta_second: bfloat16 [2048], replicated, may hold values from -4 to 4
- expand_weight: bfloat16 [2048, 8192], P('dp', 'tensor'), may hold values from -0.125 to 0.125
- expand_bias: bfloat16 [8192], P('tensor'), may hold values from -6 to 6
- reduce_weight: bfloat16 [2048, 8192], P('dp', 'tensor'), may hold values from -0.0625 to 0.0625
- reduce_bias: bfloat16 [2048], replicated, may hold values from -4 to 4
- group_sizes: int32 [32], P('dp'), may hold values from 4 to 16, as said below
- prefix_lengths: int32 [32], P('dp'), may hold values from 32 to 128, as said below
- solution_lengths: int32 [32, 16], P('dp'), may hold values from 1 to 221, as said below
- cotangent: bfloat16 [8192, 2048], P('dp'), may hold values from -6 to 6
Outputs:
- outputs: bfloat16 [8192, 2048], P('dp')
- input_gradient: bfloat16 [8192, 2048], P('dp')
- gamma_first_gradient: float32 [2048], P('dp')
- beta_first_gradient: float32 [2048], P('dp')
- heads_weight_gradient: float32 [2048, 3, 2048], P('dp', None, 'tensor')
- output_weight_gradient: float32 [2048, 2048], P('dp', 'tensor')
- output_bias_gradient: float32 [2048], P('dp')
- gamma_second_gradient: float32 [2048], P('dp')
- beta_second_gradient: float32 [2048], P('dp')
- expand_weight_gradient: float32 [2048, 8192], P('dp', 'tensor')
- expand_bias_gradient: float32 [2, 4096], P('tensor', 'dp')
- reduce_weight_gradient: float32 [2048, 8192], P('dp', 'tensor')
- reduce_bias_gradient: float32 [2048], P('dp')
Inputs may be any that keep to these rules, and one draw needn't show every extreme that they name: Each group has group_sizes solutions. `prefix_lengths`: A group's prefix and its first group_sizes solutions together take at most 256 token slots. `solution_lengths`: only a group's first group_sizes entries are used. The groups of a block fill at most 512 slots, and on at least one block exactly 512.
All inputs are finite; a program needn't handle non-finite values.
Results may differ from a plain program's by a relative error of at most 0.017.
Values may be sent and summed in bfloat16 or wider, within the bound.
No kernel may reach another device: no remote copies, remote signals or barrier semaphores. Data moves between devices by JAX's collectives and lax.ppermute only.
A program may use at most 384 MiB of HBM per device.

v0:
```python
import jax
import jax.numpy as jnp
from jax import lax
from jax.sharding import PartitionSpec as P

HEAD = 128


def layout(group_sizes, prefix_lengths, solution_lengths, row_count):
    entries = solution_lengths.shape[1]
    position = jnp.arange(entries, dtype=jnp.int32)
    counted = jnp.where(position[None, :] < group_sizes[:, None], solution_lengths, 0)
    pieces = jnp.concatenate([prefix_lengths[:, None], counted], axis=1).reshape(-1)
    bounds = jnp.cumsum(pieces)
    slot_index = jnp.arange(row_count, dtype=jnp.int32)
    piece_index = jnp.sum((slot_index[:, None] >= bounds[None, :]).astype(jnp.int32), axis=1)
    live_rows = piece_index < pieces.shape[0]
    group_index = piece_index // (entries + 1)
    opening = piece_index % (entries + 1) == 0
    same_group = (
        (group_index[:, None] == group_index[None, :]) & live_rows[:, None] & live_rows[None, :]
    )
    causal = slot_index[None, :] <= slot_index[:, None]
    visible = opening[None, :] | (piece_index[:, None] == piece_index[None, :])
    allowed = (slot_index[:, None] == slot_index[None, :]) | same_group & causal & visible
    return (allowed, live_rows)


def normalize(values, gain_vector, shift_vector):
    center = values - jnp.mean(values, axis=-1, keepdims=True)
    spread = jnp.mean(center * center, axis=-1, keepdims=True)
    return center * lax.rsqrt(spread + 1e-05) * gain_vector + shift_vector


def smooth(values):
    return jax.nn.gelu(values, approximate=True)


def body(
    inputs,
    gamma_first,
    beta_first,
    heads_weight,
    output_weight,
    output_bias,
    gamma_second,
    beta_second,
    expand_weight,
    expand_bias,
    reduce_weight,
    reduce_bias,
    group_sizes,
    prefix_lengths,
    solution_lengths,
    cotangent,
):
    row_count = inputs.shape[0]
    local_width = output_weight.shape[1]
    local_heads = local_width // HEAD
    score_scale = HEAD ** (-0.5)
    across = (((1,), (1,)), ((), ()))
    token_dims = (((0,), (0,)), ((), ()))
    allowed, live_rows = layout(group_sizes, prefix_lengths, solution_lengths, row_count)
    live_mask = live_rows.astype(jnp.float32)[:, None]
    gain_first = gamma_first.astype(jnp.float32)
    shift_first = beta_first.astype(jnp.float32)
    gain_second = gamma_second.astype(jnp.float32)
    shift_second = beta_second.astype(jnp.float32)
    residual = inputs.astype(jnp.float32)
    first_low = normalize(residual, gain_first, shift_first).astype(jnp.bfloat16)
    heads_full, output_full = (
        lax.all_gather(heads_weight, "dp", axis=0, tiled=True),
        lax.all_gather(output_weight, "dp", axis=0, tiled=True),
    )
    projected = jnp.einsum(
        "td,dch->tch", first_low, heads_full, preferred_element_type=jnp.float32
    ).astype(jnp.bfloat16)
    queries = projected[:, 0].reshape(row_count, local_heads, HEAD)
    keyset = projected[:, 1].reshape(row_count, local_heads, HEAD)
    valueset = projected[:, 2].reshape(row_count, local_heads, HEAD)

    def masked_scores():
        raw_scores = (
            jnp.einsum("qhe,khe->hqk", queries, keyset, preferred_element_type=jnp.float32)
            * score_scale
        )
        return jnp.where(allowed[None], raw_scores, -1e30)

    scores = masked_scores()
    row_peak = jnp.max(scores, axis=-1, keepdims=True)
    exponent = jnp.exp(scores - row_peak)
    row_total = jnp.sum(exponent, axis=-1, keepdims=True)
    soft_weights = exponent / row_total
    log_total = row_peak + jnp.log(row_total)
    soft_low = soft_weights.astype(jnp.bfloat16)
    mixed_heads = (
        jnp.einsum("hqk,khe->qhe", soft_low, valueset, preferred_element_type=jnp.float32)
        .reshape(row_count, local_width)
        .astype(jnp.bfloat16)
    )
    attended = lax.psum(
        lax.dot_general(mixed_heads, output_full, across, preferred_element_type=jnp.float32),
        "tensor",
    )
    middle = residual + attended + output_bias.astype(jnp.float32)
    second_low = normalize(middle, gain_second, shift_second).astype(jnp.bfloat16)
    columns = second_low
    hidden_sum = jnp.dot(
        columns,
        lax.all_gather(expand_weight, "dp", axis=0, tiled=True),
        preferred_element_type=jnp.float32,
    ) + expand_bias.astype(jnp.float32)
    hidden_low = smooth(hidden_sum).astype(jnp.bfloat16)
    branch = lax.psum(
        lax.dot_general(
            hidden_low,
            lax.all_gather(reduce_weight, "dp", axis=0, tiled=True),
            across,
            preferred_element_type=jnp.float32,
        ).astype(jnp.bfloat16),
        "tensor",
    ).astype(jnp.float32)
    outputs = (live_mask * (middle + branch + reduce_bias.astype(jnp.float32))).astype(jnp.bfloat16)
    upstream = live_mask * cotangent.astype(jnp.float32)
    reduce_bias_gradient = jnp.sum(upstream, axis=0)
    upstream_low = upstream.astype(jnp.bfloat16)
    columns = upstream_low
    hidden_tangent = jnp.dot(
        columns,
        lax.all_gather(reduce_weight, "dp", axis=0, tiled=True),
        preferred_element_type=jnp.float32,
    )
    _, smooth_pullback = jax.vjp(smooth, hidden_sum)
    sum_tangent = smooth_pullback(hidden_tangent)[0]
    expand_bias_gradient = jnp.sum(sum_tangent, axis=0)[None, :]
    sum_low = sum_tangent.astype(jnp.bfloat16)
    second_tangent = lax.psum(
        lax.dot_general(
            sum_low,
            lax.all_gather(expand_weight, "dp", axis=0, tiled=True),
            across,
            preferred_element_type=jnp.float32,
        ).astype(jnp.bfloat16),
        "tensor",
    ).astype(jnp.float32)
    feed_totals = lax.psum_scatter(
        jnp.stack(
            [
                lax.dot_general(
                    second_low, sum_low, token_dims, preferred_element_type=jnp.float32
                ),
                lax.dot_general(
                    upstream_low, hidden_low, token_dims, preferred_element_type=jnp.float32
                ),
            ],
            axis=1,
        ),
        "dp",
        scatter_dimension=0,
        tiled=True,
    )
    expand_share = feed_totals[:, 0]
    reduce_share = feed_totals[:, 1]
    _, second_pullback = jax.vjp(normalize, middle, gain_second, shift_second)
    middle_part, gamma_second_gradient, beta_second_gradient = second_pullback(second_tangent)
    middle_tangent = upstream + middle_part
    output_bias_gradient = jnp.sum(middle_tangent, axis=0)
    middle_low = middle_tangent.astype(jnp.bfloat16)
    mixed_tangent = (
        jnp.dot(middle_low, output_full, preferred_element_type=jnp.float32)
        .astype(jnp.bfloat16)
        .reshape(row_count, local_heads, HEAD)
    )
    soft_again = jnp.exp(masked_scores() - log_total)
    soft_again_low = soft_again.astype(jnp.bfloat16)
    value_tangent = jnp.einsum(
        "hqk,qhe->khe", soft_again_low, mixed_tangent, preferred_element_type=jnp.float32
    )
    weight_tangent = jnp.einsum(
        "qhe,khe->hqk", mixed_tangent, valueset, preferred_element_type=jnp.float32
    )
    score_tangent = (
        soft_again * (weight_tangent - jnp.sum(soft_again * weight_tangent, axis=-1, keepdims=True))
    ).astype(jnp.bfloat16)
    query_tangent = (
        jnp.einsum("hqk,khe->qhe", score_tangent, keyset, preferred_element_type=jnp.float32)
        * score_scale
    )
    key_tangent = (
        jnp.einsum("hqk,qhe->khe", score_tangent, queries, preferred_element_type=jnp.float32)
        * score_scale
    )
    projected_tangent = (
        jnp.stack([query_tangent, key_tangent, value_tangent], axis=1)
        .reshape(row_count, 3, local_width)
        .astype(jnp.bfloat16)
    )
    first_tangent = lax.psum(
        jnp.einsum(
            "tch,dch->td", projected_tangent, heads_full, preferred_element_type=jnp.float32
        ).astype(jnp.bfloat16),
        "tensor",
    ).astype(jnp.float32)
    heads_term = jnp.einsum(
        "tc,tkh->ckh", first_low, projected_tangent, preferred_element_type=jnp.float32
    )
    output_term = lax.dot_general(
        middle_low, mixed_heads, token_dims, preferred_element_type=jnp.float32
    )
    head_totals = lax.psum_scatter(
        jnp.concatenate([heads_term, output_term[:, None, :]], axis=1),
        "dp",
        scatter_dimension=0,
        tiled=True,
    )
    _, first_pullback = jax.vjp(normalize, residual, gain_first, shift_first)
    input_part, gamma_first_gradient, beta_first_gradient = first_pullback(first_tangent)
    input_gradient = (middle_tangent + input_part).astype(jnp.bfloat16)
    vectors = (
        lax.psum_scatter(gamma_first_gradient, "dp", scatter_dimension=0, tiled=True),
        lax.psum_scatter(beta_first_gradient, "dp", scatter_dimension=0, tiled=True),
        lax.psum_scatter(output_bias_gradient, "dp", scatter_dimension=0, tiled=True),
        lax.psum_scatter(gamma_second_gradient, "dp", scatter_dimension=0, tiled=True),
        lax.psum_scatter(beta_second_gradient, "dp", scatter_dimension=0, tiled=True),
        lax.psum_scatter(reduce_bias_gradient, "dp", scatter_dimension=0, tiled=True),
        lax.psum_scatter(expand_bias_gradient, "dp", scatter_dimension=1, tiled=True),
    )
    return (
        outputs,
        input_gradient,
        vectors[0],
        vectors[1],
        head_totals[:, :3],
        head_totals[:, 3],
        vectors[2],
        vectors[3],
        vectors[4],
        expand_share,
        vectors[6],
        reduce_share,
        vectors[5],
    )


def solution(mesh):
    placed = (
        P("dp", None),
        P(),
        P(),
        P("dp", None, "tensor"),
        P("dp", "tensor"),
        P(),
        P(),
        P(),
        P("dp", "tensor"),
        P("tensor"),
        P("dp", "tensor"),
        P(),
        P("dp"),
        P("dp"),
        P("dp", None),
        P("dp", None),
    )
    return jax.shard_map(
        body,
        mesh=mesh,
        in_specs=placed,
        out_specs=(
            P("dp", None),
            P("dp", None),
            P("dp"),
            P("dp"),
            P("dp", None, "tensor"),
            P("dp", "tensor"),
            P("dp"),
            P("dp"),
            P("dp"),
            P("dp", "tensor"),
            P("tensor", "dp"),
            P("dp", "tensor"),
            P("dp"),
        ),
        check_vma=False,
    )
```

profile of v0, /device:TPU:10, one launch (start us, length us, event | category | flops | bytes accessed | tf_op | source)
XLA Modules:
  0.0 2903.4 jit_solution(15388383072456782599)
XLA Ops:
  7.2 0.7 all-gather.5.cloned.1.call-update
  8.0 0.7 all-gather.7.cloned.1.call-update
  8.7 0.7 copy.83
  9.5 0.7 convert_element_type.107
  10.2 0.7 convert_element_type.108
  10.8 0.8 compare_select_fusion
  12.0 1.9 convert_reduce_fusion.2
  14.0 0.7 fusion.19
  15.3 0.8 fusion.41
  16.1 145.8 %all-gather.5.cloned.1.call-done = bf16[2048,3,1024]{2,0,1:T(8,128)(2,1)} async-done(((bf16[128,3,1024]{2,0,1:T(8,128)(2,1)}), bf16[2048,3,1024]{2,0,1:T(8,128)(2,1)}) %all-gather.5.cloned.1.call-update) | async-done | bytes 12582928 | tf_op jit(solution)/shard_map/all_gather | solution.py:72
  162.0 9.7 convolution_convert_fusion.2
  171.7 1.7 slice_bitcast_fusion.2
  173.5 1.2 copy.112
  174.7 1.5 copy.110
  176.2 2.7 copy.109
  178.9 2.9 fusion.66
  181.8 1.2 fusion.6
  183.0 2.2 copy-done
  185.3 2.6 fusion.34
  187.9 53.0 %all-gather.7.cloned.1.call-done = bf16[2048,1024]{1,0:T(8,128)(2,1)} async-done(((bf16[128,1024]{1,0:T(8,128)(2,1)}), bf16[2048,1024]{1,0:T(8,128)(2,1)}) %all-gather.7.cloned.1.call-update) | async-done | bytes 4194320 | tf_op jit(solution)/shard_map/all_gather | solution.py:73
  240.9 6.8 fusion.68
  249.2 26.0 all-reduce.12.cloned.1.call-done
  275.2 2.8 fusion.64
  278.0 2.0 copy-done.1
  280.6 188.2 %all-gather.9.cloned.1.call-done = bf16[2048,4096]{1,0:T(8,128)(2,1)} async-done(((bf16[128,4096]{1,0:T(8,128)(2,1)}), bf16[2048,4096]{1,0:T(8,128)(2,1)}) %all-gather.9.cloned.1.call-update) | async-done | bytes 16777232 | tf_op jit(solution)/shard_map/all_gather | solution.py:110
  468.9 15.8 fusion.61
  484.7 177.0 %all-gather.11.cloned.1.call-done = bf16[2048,4096]{1,0:T(8,128)(2,1)} async-done(((bf16[128,4096]{1,0:T(8,128)(2,1)}), bf16[2048,4096]{1,0:T(8,128)(2,1)}) %all-gather.11.cloned.1.call-update) | async-done | bytes 16777232 | tf_op jit(solution)/shard_map/all_gather | solution.py:117
  661.7 18.5 fusion.67
  680.2 1.9 copy-done.44
  682.2 13.4 convolution_convert_fusion
  695.7 2.0 copy.107
  697.7 18.8 convolution_convert_fusion.1
  716.5 0.8 all-reduce.14.cloned.1.call-done
  717.3 4.6 convert_reduce_fusion.1
  722.0 2.6 fusion.22
  724.6 2.8 fusion.62
  727.5 2.0 copy-done.8
  729.4 2.3 convolution_convert_fusion.3
  732.3 5.1 fusion.35
  737.4 4.8 multiply_reduce_fusion
  742.2 2.6 multiply_convert_fusion
  744.9 1.5 multiply_convert_fusion.3
  746.4 0.7 multiply_convert_fusion.4
  747.1 1.3 copy.99
  748.4 1.3 copy.97
  750.3 11.3 bitcast_convert_fusion
  761.8 5.1 convolution_bitcast_fusion.2
  767.0 12.0 fusion.38
  779.0 20.2 pad_maximum_fusion.1
  799.9 20.1 convolution_bitcast_fusion.1
  820.1 19.7 convolution_bitcast_fusion
  839.8 44.5 %pad_maximum_fusion = f32[2048,2,4096]{2,0,1:T(8,128)} fusion(f32[2048,1,4096]{2,0,1:T(8,128)} %convolution_bitcast_fusion, f32[2048,1,4096]{2,0,1:T(8,128)} %convolution_bitcast_fusion.1), kind=kLoop, calls=%fused_computation | loop fusion | flops 16777216 | bytes 134217728 | tf_op jit(solution)/shard_map/stack | solution.py:147
  884.4 0.6 copy-done.41
  886.3 1.5 copy.108
  887.8 2.9 convert_reduce_fusion
  890.8 2.4 fusion.23
  893.3 71.1 %all-reduce.6 = (f32[2048]{0:T(1024)S(1)}, f32[2048]{0:T(1024)S(1)}, f32[2048]{0:T(1024)S(1)}, f32[2048]{0:T(1024)S(1)}, f32[2048]{0:T(1024)S(1)}, /*index=5*/f32[2048]{0:T(1024)S(1)}) all-reduce(f32[2048]{0:T(1024)S(1)} %get-tuple-element.15, f32[2048]{0:T(1024)S(1)} %get-tuple-element.19, ...), channel_id=2, replica_groups=mesh['dp'=16,'tensor'=2] {'dp'}, use_global_device_ids=true, to_apply=%region_18.19.clone | all-reduce | flops 12288 | bytes 98304
  967.8 4.9 multiply_convert_fusion.2
  972.9 2.8 add_convert_fusion
  975.7 550.2 %reduce-scatter.6.cloned.1.call-done = f32[128,4,1024]{2,0,1:T(8,128)} async-done(((f32[2048,4,1024]{2,0,1:T(8,128)}), f32[128,4,1024]{2,0,1:T(8,128)}) %reduce-scatter.6.cloned.1.call-update) | async-done | bytes 2097168 | tf_op jit(solution)/shard_map/reduce_scatter | solution.py:210
  1525.9 2.7 slice.31
  1528.6 1.9 slice_bitcast_fusion.3
  1530.5 1360.9 %reduce-scatter.8.cloned.1.call-done = f32[128,2,4096]{2,0,1:T(8,128)} async-done(((f32[2048,2,4096]{2,0,1:T(8,128)}), f32[128,2,4096]{2,0,1:T(8,128)}) %reduce-scatter.8.cloned.1.call-update) | async-done | bytes 4194320 | tf_op jit(solution)/shard_map/reduce_scatter | solution.py:146
  2891.4 4.7 slice_bitcast_fusion
  (141 shorter events, 9.5 us)
Async XLA Ops:
  7.2 6.8 copy-start.3
  7.2 154.8 %all-gather.5.cloned.1.call-start = ((), (), s32[]{:S(2)}) async-start(), calls=%async_computation.3 | async-start | bytes 13369344 | tf_op jit(solution)/shard_map/all_gather | solution.py:72
  7.9 232.9 %all-gather.7.cloned.1.call-start = ((), (), s32[]{:S(2)}) async-start(), calls=%async_computation.4 | async-start | bytes 4456448 | tf_op jit(solution)/shard_map/all_gather | solution.py:73
  8.7 266.5 %all-reduce.12.cloned.1.call-start = ((), (), s32[]{:S(2)}) async-start(), calls=%async_computation.5 | async-start | bytes 8388608 | tf_op jit(solution)/shard_map/psum | solution.py:101
  10.2 161.6 %copy-start.21 = (f32[2048]{0:T(1024)}, f32[2048]{0:T(1024)S(1)}, u32[]{:S(2)}) copy-start(f32[2048]{0:T(1024)S(1)} %convert_element_type.107) | copy-start | bytes 24580
  10.8 160.9 %copy-start.34 = (f32[2048]{0:T(1024)}, f32[2048]{0:T(1024)S(1)}, u32[]{:S(2)}) copy-start(f32[2048]{0:T(1024)S(1)} %convert_element_type.108) | copy-start | bytes 24580
  14.0 157.7 %copy-start.23 = (f32[512]{0:T(512)}, f32[512]{0:T(512)S(1)}, u32[]{:S(2)}) copy-start(f32[512]{0:T(512)S(1)} %broadcast_multiply_fusion.1) | copy-start | bytes 6148
  14.7 0.6 copy-start.31
  14.7 157.0 %copy-start.29 = (f32[512]{0:T(512)}, f32[512]{0:T(512)S(1)}, u32[]{:S(2)}) copy-start(f32[512]{0:T(512)S(1)} %fusion.56) | copy-start | bytes 6148
  176.2 5.6 copy-start.10
  181.8 3.4 copy-start
  181.8 3.4 copy-start.13
  247.7 1.4 copy-start.38
  247.7 1.5 copy-start.39
  247.7 1.5 copy-start.40
  247.7 1.5 copy-start.33
  247.7 221.2 %all-gather.9.cloned.1.call-start = ((), (), s32[]{:S(2)}) async-start(), calls=%async_computation.6 | async-start | bytes 17825792 | tf_op jit(solution)/shard_map/all_gather | solution.py:110
  248.3 413.4 %all-gather.11.cloned.1.call-start = ((), (), s32[]{:S(2)}) async-start(), calls=%async_computation.7 | async-start | bytes 17825792 | tf_op jit(solution)/shard_map/all_gather | solution.py:117
  248.9 468.4 %all-reduce.14.cloned.1.call-start = ((), (), s32[]{:S(2)}) async-start(), calls=%async_computation.8 | async-start | bytes 4194304 | tf_op jit(solution)/shard_map/psum | solution.py:137
  249.2 219.7 %copy-start.36 = (f32[2048]{0:T(1024)}, f32[2048]{0:T(1024)S(1)}, u32[]{:S(2)}) copy-start(f32[2048]{0:T(1024)S(1)} %convert_element_type.117) | copy-start | bytes 24580
  278.0 2.1 copy-start.1
  280.6 381.1 %copy-start.14 = (bf16[512,2048]{1,0:T(8,128)(2,1)S(1)}, bf16[512,2048]{1,0:T(8,128)(2,1)}, u32[]{:S(2)}) copy-start(bf16[512,2048]{1,0:T(8,128)(2,1)} %param.31) | copy-start | bytes 6291460
  680.2 1.9 copy-start.44
  695.6 190.6 %reduce-scatter.10.cloned.1.call-start = ((), (), s32[]{:S(2)}) async-start(), calls=%async_computation.11 | async-start | bytes 2228224
  697.7 190.1 %all-reduce.16.cloned.1.call-start = ((), (), s32[]{:S(2)}) async-start(), calls=%async_computation.12 | async-start | bytes 8388608 | tf_op jit(solution)/shard_map/psum | solution.py:114
  717.3 4.6 copy-start.2
  717.3 4.7 copy-start.7
  724.6 4.8 copy-start.42
  727.5 2.0 copy-start.8
  732.3 9.9 slice-start
  737.4 4.8 slice-start.1
  742.2 2.6 copy-start.12
  744.8 1.5 copy-start.11
  748.4 1.9 copy-start.16
  750.3 11.4 copy-start.19
  761.7 5.2 copy-start.4
  761.7 5.2 copy-start.17
  761.7 5.2 copy-start.22
  761.7 5.2 copy-start.24
  761.7 5.2 copy-start.30
  761.7 5.2 copy-start.35
  761.8 764.1 %reduce-scatter.6.cloned.1.call-start = ((), (), s32[]{:S(2)}) async-start(), calls=%async_computation.9 | async-start | bytes 35651584 | tf_op jit(solution)/shard_map/reduce_scatter | solution.py:210
  761.8 5.2 copy-start.18
  761.8 5.2 copy-start.20
  799.2 0.7 copy-start.37
  799.3 2092.1 %reduce-scatter.8.cloned.1.call-start = ((), (), s32[]{:S(2)}) async-start(), calls=%async_computation.10 | async-start | bytes 71303168 | tf_op jit(solution)/shard_map/reduce_scatter | solution.py:146
  799.9 20.1 copy-start.15
  884.3 0.7 copy-start.41
  884.3 0.7 copy-start.43
  884.3 6.4 copy-start.32
  887.8 3.0 copy-start.5
  887.8 5.4 copy-start.25
  887.8 5.4 copy-start.26
  887.8 5.4 copy-start.27
  887.8 5.4 copy-start.28
  967.8 5.0 copy-start.6
  967.8 5.0 copy-start.9
Sparse Core Ops, SparseCore 0:
  10.8 151.1 all-gather.4
  164.7 76.1 all-gather.6
  247.8 27.2 all-reduce.11
  278.2 190.6 all-gather.8
  471.9 189.7 all-gather.10
  695.7 21.5 all-reduce.13
  720.2 71.8 reduce-scatter.9
  795.2 35.4 all-reduce.15
  833.2 692.6 reduce-scatter.5
  1528.2 1363.1 reduce-scatter.7
where the time goes:
time: 2910 us; the launch traced here: 2900 us
  waiting for transfers between devices  2500 us (86%)
  matrix products  171 us (6%)
  other arithmetic  101 us (3%)
  blocking collectives  71.1 us (2%)
  local copies, waits for them, and re-layouts  38.9 us (1%)
    reduce_scatter x1, waiting for transfers between devices, body(): lax.psum_scatter(jnp.stack([lax.dot_general(second_low, sum_low, token_di...  1360 us
    reduce_scatter x1, waiting for transfers between devices, body(): lax.psum_scatter(jnp.concatenate([heads_term, output_term[:, None, :]], a...  550 us
    all_gather x1, waiting for transfers between devices, body(): lax.all_gather(expand_weight, 'dp', axis=0, tiled=True)  188 us
    all_gather x1, waiting for transfers between devices, body(): lax.all_gather(reduce_weight, 'dp', axis=0, tiled=True)  177 us
    all_gather x1, waiting for transfers between devices, body(): lax.all_gather(heads_weight, 'dp', axis=0, tiled=True)  146 us
    unnamed x1, blocking collectives  71.1 us
  transfers between devices with their start and end apart: 10, of which 8 were waited for; matrix products, arithmetic and copies ran while one was open for 9% of the time, Pallas kernels for 0%

commit v1 on v0

--- a/solution.py
+++ b/solution.py
@@ -54,6 +54,26 @@
     solution_lengths,
     cotangent,
 ):
+
+    def sides_recover(block_in, row_axis, dim_at):
+        odd, v_now, s_next = (
+            lax.axis_size(row_axis),
+            lax.axis_index(row_axis),
+            block_in.shape[dim_at],
+        )
+        pool = [k0 * odd if j == dim_at else k0 for j, k0 in enumerate(block_in.shape)]
+        f_next = lax.dynamic_update_slice_in_dim(
+            jnp.zeros(pool, block_in.dtype), block_in, v_now * s_next, axis=dim_at
+        )
+        for m in range(1, odd):
+            block_in = lax.ppermute(
+                block_in, axis_name=row_axis, perm=[(j, (j + 1) % odd) for j in range(odd)]
+            )
+            f_next = lax.dynamic_update_slice_in_dim(
+                f_next, block_in, (v_now - m) % odd * s_next, axis=dim_at
+            )
+        return f_next
+
     row_count = inputs.shape[0]
     local_width = output_weight.shape[1]
     local_heads = local_width // HEAD
@@ -69,7 +89,7 @@
     residual = inputs.astype(jnp.float32)
     first_low = normalize(residual, gain_first, shift_first).astype(jnp.bfloat16)
     heads_full, output_full = (
-        lax.all_gather(heads_weight, "dp", axis=0, tiled=True),
+        sides_recover(heads_weight, "dp", 0),
         lax.all_gather(output_weight, "dp", axis=0, tiled=True),
     )
     projected = jnp.einsum(

time: 2910 us -> 3030 us (1.041)
  waiting for transfers between devices: 2500 us -> 2560 us
  starting transfers between devices: 0.58 us -> 36.1 us
  local copies, waits for them, and re-layouts: 38.9 us -> 69.9 us
    ppermute x0 -> x15, waiting for transfers between devices: none -> 230 us  [sides_recover(): lax.ppermute(block_in, axis_name=row_axis, perm=[(j, (j + 1) % odd) for j...]
    all_gather x1 -> x0, waiting for transfers between devices: 146 us -> none  [body(): lax.all_gather(heads_weight, 'dp', axis=0, tiled=True)]
    all_gather x1, waiting for transfers between devices: 53 us -> 0.01 us  [body(): lax.all_gather(output_weight, 'dp', axis=0, tiled=True)]
    ppermute x0 -> x15, starting transfers between devices: none -> 35.6 us  [sides_recover(): lax.ppermute(block_in, axis_name=row_axis, perm=[(j, (j + 1) % odd) for j...]
  transfers between devices with their start and end apart: 10 -> 24, of which waited for: 8 -> 21; matrix products, arithmetic and copies ran while one was open for 9% -> 9% of each run, Pallas kernels for 0% -> 0%
where the time goes in v1:
time: 3030 us
  waiting for transfers between devices  2560 us (84%)
  matrix products  173 us (6%)
  other arithmetic  101 us (3%)
  local copies, waits for them, and re-layouts  69.9 us (2%)
  blocking collectives  69.5 us (2%)
  starting transfers between devices  36.1 us (1%)
    reduce_scatter x1, waiting for transfers between devices, body(): lax.psum_scatter(jnp.stack([lax.dot_general(second_low, sum_low, token_di...  1360 us
    reduce_scatter x1, waiting for transfers between devices, body(): lax.psum_scatter(jnp.concatenate([heads_term, output_term[:, None, :]], a...  549 us
    ppermute x15, waiting for transfers between devices, sides_recover(): lax.ppermute(block_in, axis_name=row_axis, perm=[(j, (j + 1) % odd) for j...  230 us
    all_gather x1, waiting for transfers between devices, body(): lax.all_gather(expand_weight, 'dp', axis=0, tiled=True)  188 us
    all_gather x1, waiting for transfers between devices, body(): lax.all_gather(reduce_weight, 'dp', axis=0, tiled=True)  177 us
    unnamed x1, blocking collectives  69.5 us
  transfers between devices with their start and end apart: 24, of which 21 were waited for; matrix products, arithmetic and copies ran while one was open for 9% of the time, Pallas kernels for 0%

profile of v1, /device:TPU:10, one launch (start us, length us, event | category | flops | bytes accessed | tf_op | source)
XLA Modules:
  0.0 3025.1 jit_solution(2730310762770265056)
XLA Ops:
  8.8 18.0 collective-permute-done
  26.8 2.4 collective-permute-start.1
  29.2 16.6 collective-permute-done.1
  45.8 2.7 collective-permute-start.2
  48.5 16.6 collective-permute-done.2
  66.9 16.6 collective-permute-done.3
  84.6 16.3 collective-permute-done.4
  102.1 16.5 collective-permute-done.5
  119.5 16.8 collective-permute-done.6
  137.2 15.2 collective-permute-done.7
  153.8 17.0 collective-permute-done.8
  171.5 17.0 collective-permute-done.9
  194.7 13.4 collective-permute-done.10
  208.1 3.1 collective-permute-start.11
  212.7 19.9 collective-permute-done.11
  232.6 8.2 collective-permute-start.12
  240.8 6.1 broadcast_in_dim.38
  250.6 4.8 collective-permute-done.12
  255.3 7.8 collective-permute-start.13
  268.8 23.5 collective-permute-done.13
  292.3 4.6 collective-permute-start.14
  296.9 2.1 constant_dynamic-update-slice_fusion.6
  298.9 2.1 constant_dynamic-update-slice_fusion.5
  301.0 2.1 constant_dynamic-update-slice_fusion.4
  303.1 2.1 constant_dynamic-update-slice_fusion.3
  305.2 2.1 constant_dynamic-update-slice_fusion.2
  310.8 9.8 convolution_convert_fusion.2
  325.1 2.7 copy.109
  327.7 2.9 fusion.66
  331.9 2.2 copy-done
  334.1 2.6 fusion.34
  336.7 6.9 fusion.68
  345.3 51.9 %all-reduce.12.cloned.1.call-done = f32[512,2048]{1,0:T(8,128)} async-done(((f32[512,2048]{1,0:T(8,128)}), f32[512,2048]{1,0:T(8,128)}) %all-reduce.12.cloned.1.call-update) | async-done | bytes 4194320 | tf_op jit(solution)/shard_map/psum | solution.py:121
  397.2 2.8 fusion.64
  400.0 2.0 copy-done.1
  402.6 188.4 %all-gather.6.cloned.1.call-done = bf16[2048,4096]{1,0:T(8,128)(2,1)} async-done(((bf16[128,4096]{1,0:T(8,128)(2,1)}), bf16[2048,4096]{1,0:T(8,128)(2,1)}) %all-gather.6.cloned.1.call-update) | async-done | bytes 16777232 | tf_op jit(solution)/shard_map/all_gather | solution.py:130
  591.0 15.8 fusion.61
  606.8 177.1 %all-gather.8.cloned.1.call-done = bf16[2048,4096]{1,0:T(8,128)(2,1)} async-done(((bf16[128,4096]{1,0:T(8,128)(2,1)}), bf16[2048,4096]{1,0:T(8,128)(2,1)}) %all-gather.8.cloned.1.call-update) | async-done | bytes 16777232 | tf_op jit(solution)/shard_map/all_gather | solution.py:137
  783.9 18.5 fusion.67
  804.4 13.4 convolution_convert_fusion
  819.9 18.8 convolution_convert_fusion.1
  839.5 4.6 convert_reduce_fusion.1
  844.2 2.6 fusion.22
  846.8 2.9 fusion.62
  851.7 2.3 convolution_convert_fusion.3
  854.6 6.1 fusion.35
  860.7 4.7 multiply_reduce_fusion
  865.4 2.6 multiply_convert_fusion
  875.1 11.0 bitcast_convert_fusion
  886.2 5.1 convolution_bitcast_fusion.2
  891.4 12.2 fusion.38
  903.5 20.3 pad_maximum_fusion.1
  924.5 20.1 convolution_bitcast_fusion.1
  944.6 20.2 convolution_bitcast_fusion
  964.8 44.5 %pad_maximum_fusion = f32[2048,2,4096]{2,0,1:T(8,128)} fusion(f32[2048,1,4096]{2,0,1:T(8,128)} %convolution_bitcast_fusion, f32[2048,1,4096]{2,0,1:T(8,128)} %convolution_bitcast_fusion.1), kind=kLoop, calls=%fused_computation | loop fusion | flops 16777216 | bytes 134217728 | tf_op jit(solution)/shard_map/stack | solution.py:167
  1012.9 2.9 convert_reduce_fusion
  1015.8 2.4 fusion.23
  1018.3 69.5 %all-reduce.6 = (f32[2048]{0:T(1024)S(1)}, f32[2048]{0:T(1024)S(1)}, f32[2048]{0:T(1024)S(1)}, f32[2048]{0:T(1024)S(1)}, f32[2048]{0:T(1024)S(1)}, /*index=5*/f32[2048]{0:T(1024)S(1)}) all-reduce(f32[2048]{0:T(1024)S(1)} %get-tuple-element.15, f32[2048]{0:T(1024)S(1)} %get-tuple-element.19, ...), channel_id=2, replica_groups=mesh['dp'=16,'tensor'=2] {'dp'}, use_global_device_ids=true, to_apply=%region_18.19.clone | all-reduce | flops 12288 | bytes 98304
  1091.3 5.0 multiply_convert_fusion.2
  1096.4 2.8 add_convert_fusion
  1099.2 548.7 %reduce-scatter.6.cloned.1.call-done = f32[128,4,1024]{2,0,1:T(8,128)} async-done(((f32[2048,4,1024]{2,0,1:T(8,128)}), f32[128,4,1024]{2,0,1:T(8,128)}) %reduce-scatter.6.cloned.1.call-update) | async-done | bytes 2097168 | tf_op jit(solution)/shard_map/reduce_scatter | solution.py:230
  1648.0 2.7 slice.31
  1652.6 1361.1 %reduce-scatter.8.cloned.1.call-done = f32[128,2,4096]{2,0,1:T(8,128)} async-done(((f32[2048,2,4096]{2,0,1:T(8,128)}), f32[128,2,4096]{2,0,1:T(8,128)}) %reduce-scatter.8.cloned.1.call-update) | async-done | bytes 4194320 | tf_op jit(solution)/shard_map/reduce_scatter | solution.py:166
  3013.7 4.7 slice_bitcast_fusion
  (219 shorter events, 61.3 us)
Async XLA Ops:
  7.2 204.1 %copy-start.3 = (bf16[512,2048]{1,0:T(8,128)(2,1)S(1)}, bf16[512,2048]{1,0:T(8,128)(2,1)}, u32[]{:S(2)}) copy-start(bf16[512,2048]{1,0:T(8,128)(2,1)} %param.16) | copy-start | bytes 6291460
  7.2 329.5 %all-gather.4.cloned.1.call-start = ((), (), s32[]{:S(2)}) async-start(), calls=%async_computation.3 | async-start | bytes 4456448 | tf_op jit(solution)/shard_map/all_gather | solution.py:93
  7.2 19.5 collective-permute-start
  26.8 56.7 %copy-start.24 = (bf16[128,3,1024]{2,0,1:T(8,128)(2,1)}, bf16[128,3,1024]{2,0,1:T(8,128)(2,1)S(1)}, u32[]{:S(2)}) copy-start(bf16[128,3,1024]{2,0,1:T(8,128)(2,1)S(1)} %collective-permute-done) | copy-start | bytes 2359300
  26.8 19.0 collective-permute-start.1
  45.8 19.3 collective-permute-start.2
  65.1 18.4 collective-permute-start.3
  83.4 17.4 collective-permute-start.4
  101.8 16.8 collective-permute-start.5
  119.5 16.8 collective-permute-start.6
  137.2 15.2 collective-permute-start.7
  153.3 17.5 collective-permute-start.8
  170.8 17.7 collective-permute-start.9
  171.4 225.7 %all-reduce.12.cloned.1.call-start = ((), (), s32[]{:S(2)}) async-start(), calls=%async_computation.4 | async-start | bytes 8388608 | tf_op jit(solution)/shard_map/psum | solution.py:121
  188.5 19.6 collective-permute-start.10
  190.8 120.0 %copy-start.38 = (f32[2048]{0:T(1024)}, f32[2048]{0:T(1024)S(1)}, u32[]{:S(2)}) copy-start(f32[2048]{0:T(1024)S(1)} %convert_element_type.107) | copy-start | bytes 24580
  191.5 119.3 %copy-start.51 = (f32[2048]{0:T(1024)}, f32[2048]{0:T(1024)S(1)}, u32[]{:S(2)}) copy-start(f32[2048]{0:T(1024)S(1)} %convert_element_type.108) | copy-start | bytes 24580
  194.7 116.1 %copy-start.40 = (f32[512]{0:T(512)}, f32[512]{0:T(512)S(1)}, u32[]{:S(2)}) copy-start(f32[512]{0:T(512)S(1)} %broadcast_multiply_fusion.1) | copy-start | bytes 6148
  208.1 24.5 collective-permute-start.11
  212.6 98.2 %copy-start.46 = (f32[512]{0:T(512)}, f32[512]{0:T(512)S(1)}, u32[]{:S(2)}) copy-start(f32[512]{0:T(512)S(1)} %fusion.56) | copy-start | bytes 6148
  212.6 34.3 %copy-start.23 = (bf16[128,3,1024]{2,0,1:T(8,128)(2,1)S(1)}, bf16[128,3,1024]{2,0,1:T(8,128)(2,1)}, u32[]{:S(2)}) copy-start(bf16[128,3,1024]{2,0,1:T(8,128)(2,1)} %param.19) | copy-start | bytes 2359300
  212.6 36.0 %copy-start.25 = (bf16[128,3,1024]{2,0,1:T(8,128)(2,1)S(1)}, bf16[128,3,1024]{2,0,1:T(8,128)(2,1)}, u32[]{:S(2)}) copy-start(bf16[128,3,1024]{2,0,1:T(8,128)(2,1)} %copy-done.24) | copy-start | bytes 2359300
  212.6 37.0 %copy-start.29 = (bf16[128,3,1024]{2,0,1:T(8,128)(2,1)S(1)}, bf16[128,3,1024]{2,0,1:T(8,128)(2,1)}, u32[]{:S(2)}) copy-start(bf16[128,3,1024]{2,0,1:T(8,128)(2,1)} %copy-done.28) | copy-start | bytes 2359300
  232.6 22.7 collective-permute-start.12
  246.9 17.2 copy-start.27
  246.9 18.2 copy-start.31
  247.8 18.2 copy-start.33
  249.6 17.3 copy-start.35
  250.6 17.3 copy-start.37
  255.3 37.0 %collective-permute-start.13 = (bf16[128,3,1024]{2,0,1:T(8,128)(2,1)}, bf16[128,3,1024]{2,0,1:T(8,128)(2,1)S(1)}, u32[]{:S(2)}, u32[]{:S(2)}) collective-permute-start(bf16[128,3,1024]{2,0,1:T(8,128)(2,1)} %collective-permute-done.12), channel_id=1, source_target_pairs={{0,2},{2,4},{4,6},{6,8},{8,10},{10,12},{12,14},{14,16},{16,18},{18... | collective-permute-start | bytes 2359304 | tf_op jit(solution)/shard_map/ppermute | solution.py:69
  292.3 17.6 collective-permute-start.14
  325.1 5.6 copy-start.10
  343.6 247.4 %all-gather.6.cloned.1.call-start = ((), (), s32[]{:S(2)}) async-start(), calls=%async_computation.5 | async-start | bytes 17825792 | tf_op jit(solution)/shard_map/all_gather | solution.py:130
  344.4 439.5 %all-gather.8.cloned.1.call-start = ((), (), s32[]{:S(2)}) async-start(), calls=%async_computation.6 | async-start | bytes 17825792 | tf_op jit(solution)/shard_map/all_gather | solution.py:137
  345.0 494.5 %all-reduce.14.cloned.1.call-start = ((), (), s32[]{:S(2)}) async-start(), calls=%async_computation.7 | async-start | bytes 4194304 | tf_op jit(solution)/shard_map/psum | solution.py:157
  345.2 245.8 %copy-start.53 = (f32[2048]{0:T(1024)}, f32[2048]{0:T(1024)S(1)}, u32[]{:S(2)}) copy-start(f32[2048]{0:T(1024)S(1)} %convert_element_type.117) | copy-start | bytes 24580
  402.6 381.3 %copy-start.15 = (bf16[512,2048]{1,0:T(8,128)(2,1)S(1)}, bf16[512,2048]{1,0:T(8,128)(2,1)}, u32[]{:S(2)}) copy-start(bf16[512,2048]{1,0:T(8,128)(2,1)} %param.31) | copy-start | bytes 6291460
  817.8 193.5 %reduce-scatter.10.cloned.1.call-start = ((), (), s32[]{:S(2)}) async-start(), calls=%async_computation.10 | async-start | bytes 2228224
  819.9 193.0 %all-reduce.16.cloned.1.call-start = ((), (), s32[]{:S(2)}) async-start(), calls=%async_computation.11 | async-start | bytes 8388608 | tf_op jit(solution)/shard_map/psum | solution.py:134
  839.5 4.6 copy-start.2
  839.5 4.7 copy-start.7
  846.8 4.9 copy-start.59
  854.6 10.8 slice-start
  860.7 4.8 slice-start.1
  871.8 14.2 copy-start.18
  873.7 12.3 copy-start.20
  886.1 5.2 copy-start.4
  886.1 5.2 copy-start.19
  886.1 5.2 copy-start.39
  886.1 5.2 copy-start.41
  886.1 5.2 copy-start.47
  886.1 5.2 copy-start.52
  886.2 761.8 %reduce-scatter.6.cloned.1.call-start = ((), (), s32[]{:S(2)}) async-start(), calls=%async_computation.8 | async-start | bytes 35651584 | tf_op jit(solution)/shard_map/reduce_scatter | solution.py:230
  886.2 5.2 copy-start.21
  886.2 5.2 copy-start.22
  923.8 2089.8 %reduce-scatter.8.cloned.1.call-start = ((), (), s32[]{:S(2)}) async-start(), calls=%async_computation.9 | async-start | bytes 71303168 | tf_op jit(solution)/shard_map/reduce_scatter | solution.py:166
  924.5 20.1 copy-start.17
  1009.4 6.4 copy-start.49
  1012.9 5.4 copy-start.42
  1012.9 5.4 copy-start.43
  1012.9 5.4 copy-start.44
  1012.9 5.4 copy-start.45
  1091.3 5.0 copy-start.6
  1091.3 5.1 copy-start.9
  (24 other events, 40.9 us)
Sparse Core Ops, SparseCore 0:
  171.6 132.7 all-gather.3
  343.8 53.3 all-reduce.11
  400.3 190.6 all-gather.5
  594.0 189.7 all-gather.7
  817.9 21.5 all-reduce.13
  842.2 72.1 reduce-scatter.9
  917.4 35.3 all-reduce.15
  955.3 692.5 reduce-scatter.5
  1650.4 1363.1 reduce-scatter.7
